TPU v7x, 256 devices: a whole 4x4x8 slice. The times are simulated.
256 devices in a mesh: seq: 64 (over y, z, core), tp: 4 (over x).
Axes of the slice: x: 4, y: 4, z: 8, core: 2. Of those that a mesh axis runs over, the one named last changes fastest.
Arguments:
- inputs: bfloat16 [4, 4, 1024], P(None, None, 'tp'), may hold values from -64 to 64
- attention_gain: bfloat16 [1024], replicated, may hold values from 0.099609375 to 1.8984375
- forward_gain: bfloat16 [1024], replicated, may hold values from 0.099609375 to 1.8984375
- query_weight: bfloat16 [1024, 1024], P(None, 'tp'), may hold values from -0.1875 to 0.1875
- key_weight: bfloat16 [1024, 1024], P(None, 'tp'), may hold values from -0.1875 to 0.1875
- value_weight: bfloat16 [1024, 1024], P(None, 'tp'), may hold values from -0.1875 to 0.1875
- output_weight: bfloat16 [1024, 1024], P('tp'), may hold values from -0.1875 to 0.1875
- gate_weight: bfloat16 [1024, 4096], P(None, 'tp'), may hold values from -0.1875 to 0.1875
- up_weight: bfloat16 [1024, 4096], P(None, 'tp'), may hold values from -0.1875 to 0.1875
- down_weight: bfloat16 [4096, 1024], P('tp'), may hold values from -0.09375 to 0.09375
- variate_bias: float32 [2, 16], replicated, may hold values from -256 to 256
- cache_keys: bfloat16 [4, 32768, 1024], P(None, 'seq', 'tp'), may hold values from -15 to 15
- cache_values: bfloat16 [4, 32768, 1024], P(None, 'seq', 'tp'), may hold values from -12 to 12
- cache_variates: int32 [4, 32768], P(None, 'seq'), may hold values from 0 to 7
- cache_mask: int32 [4, 32768], P(None, 'seq'), may hold values 0 or 1
- cache_lengths: int32 [4], replicated, may hold values from 1 to 32768, as said below
- fresh_flags: int32 [4], replicated, may hold values 0 or 1
- new_variates: int32 [4, 4], replicated, may hold values from 0 to 7
- new_times: int32 [4, 4], replicated, may hold values from 0 to 32771
Outputs:
- hidden_states: bfloat16 [4, 4, 1024], P(None, None, 'tp')
- new_keys: bfloat16 [4, 4, 1024], P(None, None, 'tp')
- new_values: bfloat16 [4, 4, 1024], P(None, None, 'tp')
Inputs may be any that keep to these rules, and one draw needn't show every extreme that they name: `cache_lengths`: some request has exactly 32768 filled positions.
All inputs are finite; a program needn't handle non-finite values. No bound on the sum of `cache_mask` on one device may be relied on, other than what follows from the above.
Results may differ from a plain program's by a relative error of at most 0.014.
Values may be sent and summed in bfloat16 or wider, within the bound.
A program may use at most 64 MiB of HBM per device.

v0:
```python
import math
import jax
import jax.numpy as jnp
from jax import lax
from jax.sharding import PartitionSpec as P

D = 1024
HEAD_DIM = 64
STEPS = 4
epsilon = 1e-05


def rotated(blocks, times):
    half = blocks.shape[-1] // 2
    ladder = jnp.arange(half, dtype=jnp.float32) * (2.0 / blocks.shape[-1])
    inverse = jnp.exp(-math.log(10000.0) * ladder)
    angles = times.astype(jnp.float32)[:, None] * inverse[None, :]
    cosine = jnp.cos(angles)[:, None, :]
    sine = jnp.sin(angles)[:, None, :]
    first = blocks[..., :half]
    second = blocks[..., half:]
    return jnp.concatenate(
        [first * cosine - second * sine, second * cosine + first * sine], axis=-1
    )


def join_parts(earlier, later):
    peak = jnp.maximum(earlier[0], later[0])
    factor_one = jnp.exp(earlier[0] - peak)
    factor_two = jnp.exp(later[0] - peak)
    totals = earlier[1] * factor_one + later[1] * factor_two
    repeat_by = earlier[2].shape[-1] // earlier[0].shape[-1]
    sums = earlier[2] * jnp.repeat(factor_one, repeat_by, axis=1) + later[2] * jnp.repeat(
        factor_two, repeat_by, axis=1
    )
    return (peak, totals, sums)


def on_device(
    inputs,
    attention_gain,
    forward_gain,
    query_weight,
    key_weight,
    value_weight,
    output_weight,
    gate_weight,
    up_weight,
    down_weight,
    variate_bias,
    cache_keys,
    cache_values,
    cache_variates,
    cache_mask,
    cache_lengths,
    fresh_flags,
    new_variates,
    new_times,
):
    local_width = query_weight.shape[1]
    local_heads = local_width // HEAD_DIM
    requests = inputs.shape[0]
    columns = inputs.shape[2]
    span = cache_keys.shape[1]
    scale = 1.0 / math.sqrt(HEAD_DIM)
    column_start = lax.axis_index("tp") * columns
    head_start = lax.axis_index("tp") * local_heads
    bias_local = lax.dynamic_slice_in_dim(variate_bias, head_start, local_heads, 1)
    same_bias = bias_local[0]
    other_bias = bias_local[1]
    positions = lax.axis_index("seq") * span + jnp.arange(span, dtype=jnp.int32)
    usable = (
        (positions[None, :] < cache_lengths[:, None])
        & (cache_mask == 1)
        & (fresh_flags[:, None] == 0)
    )
    key_blocks = cache_keys.reshape(requests, span, local_heads, HEAD_DIM)
    value_blocks = cache_values.reshape(requests, span, local_heads, HEAD_DIM)
    gain_first = attention_gain.astype(jnp.float32)[None, :]
    gain_second = forward_gain.astype(jnp.float32)[None, :]
    gain_first_local = lax.dynamic_slice_in_dim(gain_first, column_start, columns, 1)
    gain_second_local = lax.dynamic_slice_in_dim(gain_second, column_start, columns, 1)
    hidden_list = []
    key_list = []
    value_list = []
    for step_index in range(STEPS):
        current_low = inputs[:, step_index, :]
        current_local = current_low.astype(jnp.float32)
        square_sum = lax.psum(jnp.sum(current_local * current_local, axis=1), "tp")
        inverse_rms = lax.rsqrt(square_sum / D + epsilon)
        normed_local = (current_local * inverse_rms[:, None] * gain_first_local).astype(
            jnp.bfloat16
        )
        normed = lax.all_gather(normed_local, "tp", axis=1, tiled=True)
        query_full = jnp.dot(normed, query_weight, preferred_element_type=jnp.float32)
        key_full = jnp.dot(normed, key_weight, preferred_element_type=jnp.float32)
        value_full = jnp.dot(normed, value_weight, preferred_element_type=jnp.float32)
        times_now = new_times[:, step_index]
        queries_now = rotated(
            query_full.reshape(requests, local_heads, HEAD_DIM), times_now
        ).astype(jnp.bfloat16)
        keys_now = rotated(key_full.reshape(requests, local_heads, HEAD_DIM), times_now).astype(
            jnp.bfloat16
        )
        values_now = value_full.reshape(requests, local_heads, HEAD_DIM).astype(jnp.bfloat16)
        key_list.append(keys_now)
        value_list.append(values_now)
        variate_now = new_variates[:, step_index]
        same_cache = cache_variates == variate_now[:, None]
        scores = (
            jnp.einsum("rhe,rche->rhc", queries_now, key_blocks, preferred_element_type=jnp.float32)
            * scale
        )
        scores = scores + jnp.where(
            same_cache[:, None, :], same_bias[None, :, None], other_bias[None, :, None]
        )
        scores = jnp.where(usable[:, None, :], scores, -1e30)
        local_peak = jnp.max(scores, axis=2)
        raw = jnp.where(usable[:, None, :], jnp.exp(scores - local_peak[:, :, None]), 0.0)
        local_total = jnp.sum(raw, axis=2)
        local_sum = jnp.einsum(
            "rhc,rche->rhe",
            raw.astype(jnp.bfloat16),
            value_blocks,
            preferred_element_type=jnp.float32,
        ).reshape(requests, local_width)
        peak_all = lax.pmax(local_peak, "seq")
        factor = jnp.exp(local_peak - peak_all)
        totals_all, sums_all = lax.psum(
            (local_total * factor, local_sum * jnp.repeat(factor, HEAD_DIM, axis=1)), "seq"
        )
        merged = (peak_all, totals_all, sums_all)
        fresh_keys = jnp.stack(key_list, axis=1)
        fresh_values = jnp.stack(value_list, axis=1)
        same_new = new_variates[:, : step_index + 1] == variate_now[:, None]
        new_scores = (
            jnp.einsum("rhe,rshe->rhs", queries_now, fresh_keys, preferred_element_type=jnp.float32)
            * scale
        )
        new_scores = new_scores + jnp.where(
            same_new[:, None, :], same_bias[None, :, None], other_bias[None, :, None]
        )
        new_peak = jnp.max(new_scores, axis=2)
        new_raw = jnp.exp(new_scores - new_peak[:, :, None])
        new_total = jnp.sum(new_raw, axis=2)
        new_sum = jnp.einsum(
            "rhs,rshe->rhe",
            new_raw.astype(jnp.bfloat16),
            fresh_values,
            preferred_element_type=jnp.float32,
        ).reshape(requests, local_width)
        joined = join_parts(merged, (new_peak, new_total, new_sum))
        attention = (joined[2] / jnp.repeat(joined[1], HEAD_DIM, axis=1)).astype(jnp.bfloat16)
        partial_out = jnp.dot(attention, output_weight, preferred_element_type=jnp.float32)
        projected_local = lax.psum_scatter(partial_out, "tp", scatter_dimension=1, tiled=True)
        middle_local = (current_local + projected_local).astype(jnp.bfloat16).astype(jnp.float32)
        middle_sum = lax.psum(jnp.sum(middle_local * middle_local, axis=1), "tp")
        second_rms = lax.rsqrt(middle_sum / D + epsilon)
        normed_two_local = (middle_local * second_rms[:, None] * gain_second_local).astype(
            jnp.bfloat16
        )
        normed_two = lax.all_gather(normed_two_local, "tp", axis=1, tiled=True)
        gate_part = jnp.dot(normed_two, gate_weight, preferred_element_type=jnp.float32)
        up_part = jnp.dot(normed_two, up_weight, preferred_element_type=jnp.float32)
        activated = (jax.nn.silu(gate_part) * up_part).astype(jnp.bfloat16)
        down_part = jnp.dot(activated, down_weight, preferred_element_type=jnp.float32)
        forward = lax.psum_scatter(down_part, "tp", scatter_dimension=1, tiled=True)
        hidden_list.append((middle_local + forward).astype(jnp.bfloat16))
    hidden_states = jnp.stack(hidden_list, axis=1)
    new_keys = jnp.stack(key_list, axis=1).reshape(requests, STEPS, local_width)
    new_values = jnp.stack(value_list, axis=1).reshape(requests, STEPS, local_width)
    return (hidden_states, new_keys, new_values)


def solution(mesh):
    return jax.shard_map(
        on_device,
        mesh=mesh,
        in_specs=(
            P(None, None, "tp"),
            P(),
            P(),
            P(None, "tp"),
            P(None, "tp"),
            P(None, "tp"),
            P("tp", None),
            P(None, "tp"),
            P(None, "tp"),
            P("tp", None),
            P(),
            P(None, "seq", "tp"),
            P(None, "seq", "tp"),
            P(None, "seq"),
            P(None, "seq"),
            P(),
            P(),
            P(),
            P(),
        ),
        out_specs=(P(None, None, "tp"), P(None, None, "tp"), P(None, None, "tp")),
        check_vma=False,
    )
```

profile of v0, /device:TPU:8, one launch (start us, length us, event | category | flops | bytes accessed | tf_op | source)
XLA Modules:
  0.0 712.5 jit_solution(17226373592038998446)
XLA Ops:
  7.3 0.9 fusion.172
  8.7 10.5 %all-reduce.3 = (f32[4]{0:T(128)S(1)}, f32[4]{0:T(128)S(1)}, f32[4]{0:T(128)S(1)}, f32[4]{0:T(128)S(1)}) all-reduce(f32[4]{0:T(128)S(1)} %fusion.94, f32[4]{0:T(128)S(1)} %fusion.106, f32[4]{0:T(128)S(1)} %fusion.102, f32[4]{0:T(128)S(1)} %fusion.98), channel_id=1, replica_groups=mesh['seq'=64,'tp'=4] {'tp'}, use_global_device_ids=true, to_apply=%region_1.0 | all-reduce | flops 16 | bytes 128 | tf_op jit(solution)/shard_map/psum | solution.py:89
  19.2 0.8 dynamic-slice.6
  20.1 10.4 %all_gather.24 = bf16[4,1024]{1,0:T(4,128)(2,1)S(1)} all-gather(bf16[4,256]{1,0:T(4,128)(2,1)S(1)} %get-tuple-element.136), channel_id=1, replica_groups=mesh['seq'=64,'tp'=4] {'tp'}, dimensions={1}, use_global_device_ids=true | all-gather | bytes 10240 | tf_op jit(solution)/shard_map/all_gather | solution.py:94
  30.5 1.2 convolution_convert_fusion.3
  31.7 1.2 fusion.174
  32.9 10.5 %all_gather.26 = bf16[4,1024]{1,0:T(4,128)(2,1)S(1)} all-gather(bf16[4,256]{1,0:T(4,128)(2,1)S(1)} %get-tuple-element.137), channel_id=1, replica_groups=mesh['seq'=64,'tp'=4] {'tp'}, dimensions={1}, use_global_device_ids=true | all-gather | bytes 10240 | tf_op jit(solution)/shard_map/all_gather | solution.py:94
  43.4 1.2 convolution_convert_fusion.2
  44.6 1.2 fusion.177
  46.2 10.4 %all_gather.28 = bf16[4,1024]{1,0:T(4,128)(2,1)S(1)} all-gather(bf16[4,256]{1,0:T(4,128)(2,1)S(1)} %get-tuple-element.138), channel_id=1, replica_groups=mesh['seq'=64,'tp'=4] {'tp'}, dimensions={1}, use_global_device_ids=true | all-gather | bytes 10240 | tf_op jit(solution)/shard_map/all_gather | solution.py:94
  57.1 10.5 %all_gather.30 = bf16[4,1024]{1,0:T(4,128)(2,1)S(1)} all-gather(bf16[4,256]{1,0:T(4,128)(2,1)S(1)} %get-tuple-element.139), channel_id=1, replica_groups=mesh['seq'=64,'tp'=4] {'tp'}, dimensions={1}, use_global_device_ids=true | all-gather | bytes 10240 | tf_op jit(solution)/shard_map/all_gather | solution.py:94
  68.5 0.2 slice_reduce_fusion.3
  70.6 1.5 copy.47
  72.6 0.3 fusion.65
  73.0 0.2 fusion.68
  73.3 0.2 fusion.71
  73.6 0.2 fusion.53
  73.9 1.5 copy.48
  75.6 0.2 fusion.169
  75.8 108.2 %all-reduce.1 = (f32[4,4]{1,0:T(4,128)S(1)}, f32[4,4]{1,0:T(4,128)S(1)}, f32[4,4]{1,0:T(4,128)S(1)}, f32[4,4]{1,0:T(4,128)S(1)}) all-reduce(f32[4,4]{1,0:T(4,128)S(1)} %get-tuple-element.78, f32[4,4]{1,0:T(4,128)S(1)} %get-tuple-element.125, f32[4,4]{1,0:T(4,128)S(1)} %get-tuple-element.123, ...), channel_id=1, replica_groups=mesh['seq'=64,'tp'=4] {'seq'}, use_global_device_ids=true, to_apply=%region_40.41 | all-reduce | flops 64 | bytes 512 | tf_op jit(solution)/shard_map/pmax | solution.py:127
  184.0 0.2 fusion.20
  184.2 0.4 fusion.12
  184.6 1.7 fusion.14
  186.3 1.6 fusion.16
  187.9 0.4 fusion.18
  189.5 231.8 %all-reduce = (f32[4,4]{1,0:T(4,128)S(1)}, f32[4,256]{1,0:T(4,128)S(1)}, f32[4,4]{1,0:T(4,128)S(1)}, f32[4,256]{1,0:T(4,128)S(1)}, f32[4,4]{1,0:T(4,128)S(1)}, /...) all-reduce(f32[4,4]{1,0:T(4,128)S(1)} %get-tuple-element.70, ...), channel_id=1, replica_groups=mesh['seq'=64,'tp'=4] {'seq'}, use_global_device_ids=true, to_apply=%region_44.45 | all-reduce | flops 4160 | bytes 33280 | tf_op jit(solution)/shard_map/psum | solution.py:129
  421.8 1.2 convolution_bitcast_fusion.4
  424.5 1.2 convolution_bitcast_fusion.5
  427.2 1.2 convolution_bitcast_fusion.6
  429.2 1.1 convolution_bitcast_fusion.7
  430.8 0.6 copy.56
  431.4 0.6 copy.55
  432.0 43.5 %reduce-scatter.37.cloned.1.call-done = f32[256,4]{1,0:T(8,128)} async-done(((f32[1024,4]{1,0:T(8,128)}), f32[256,4]{1,0:T(8,128)}) %reduce-scatter.37.cloned.1.call-update) | async-done | bytes 4112
  475.5 1.0 copy.105
  476.5 25.3 %reduce-scatter.33.cloned.1.call-done = f32[256,4]{1,0:T(8,128)} async-done(((f32[1024,4]{1,0:T(8,128)}), f32[256,4]{1,0:T(8,128)}) %reduce-scatter.33.cloned.1.call-update) | async-done | bytes 4112
  501.8 1.0 copy.101
  502.7 25.3 %reduce-scatter.29.cloned.1.call-done = f32[256,4]{1,0:T(8,128)} async-done(((f32[1024,4]{1,0:T(8,128)}), f32[256,4]{1,0:T(8,128)}) %reduce-scatter.29.cloned.1.call-update) | async-done | bytes 4112
  528.1 1.0 copy.97
  529.0 25.2 %reduce-scatter.25.cloned.1.call-done = f32[256,4]{1,0:T(8,128)} async-done(((f32[1024,4]{1,0:T(8,128)}), f32[256,4]{1,0:T(8,128)}) %reduce-scatter.25.cloned.1.call-update) | async-done | bytes 4112
  554.2 1.0 copy.93
  555.5 8.4 %all-reduce.2 = (f32[4]{0:T(128)S(1)}, f32[4]{0:T(128)S(1)}, f32[4]{0:T(128)S(1)}, f32[4]{0:T(128)S(1)}) all-reduce(f32[4]{0:T(128)S(1)} %get-tuple-element.156, f32[4]{0:T(128)S(1)} %get-tuple-element.54, f32[4]{0:T(128)S(1)} %get-tuple-element.154, f32[4]{0:T(128)S(1)} %get-tuple-element.47), channel_id=1, replica_groups=mesh['seq'=64,'tp'=4] {'tp'}, use_global_device_ids=true, to_apply=%region_48.49 | all-reduce | flops 16 | bytes 128 | tf_op jit(solution)/shard_map/psum | solution.py:157
  564.0 10.4 %all_gather.25 = bf16[4,1024]{1,0:T(4,128)(2,1)S(1)} all-gather(bf16[4,256]{1,0:T(4,128)(2,1)S(1)} %get-tuple-element.130), channel_id=1, replica_groups=mesh['seq'=64,'tp'=4] {'tp'}, dimensions={1}, use_global_device_ids=true | all-gather | bytes 10240 | tf_op jit(solution)/shard_map/all_gather | solution.py:162
  574.4 10.4 %all_gather.27 = bf16[4,1024]{1,0:T(4,128)(2,1)S(1)} all-gather(bf16[4,256]{1,0:T(4,128)(2,1)S(1)} %get-tuple-element.131), channel_id=1, replica_groups=mesh['seq'=64,'tp'=4] {'tp'}, dimensions={1}, use_global_device_ids=true | all-gather | bytes 10240 | tf_op jit(solution)/shard_map/all_gather | solution.py:162
  584.8 10.4 %all_gather.29 = bf16[4,1024]{1,0:T(4,128)(2,1)S(1)} all-gather(bf16[4,256]{1,0:T(4,128)(2,1)S(1)} %get-tuple-element.132), channel_id=1, replica_groups=mesh['seq'=64,'tp'=4] {'tp'}, dimensions={1}, use_global_device_ids=true | all-gather | bytes 10240 | tf_op jit(solution)/shard_map/all_gather | solution.py:162
  595.2 0.4 fusion.181
  595.6 0.4 fusion.178
  596.0 0.4 fusion.175
  596.3 4.1 convolution_bitcast_fusion.3
  600.5 0.2 reduce-scatter.31.cloned.1.call-start
  600.7 4.1 convolution_bitcast_fusion.2
  604.8 4.1 convolution_bitcast_fusion.1
  608.8 10.5 %all_gather.31 = bf16[4,1024]{1,0:T(4,128)(2,1)S(1)} all-gather(bf16[4,256]{1,0:T(4,128)(2,1)S(1)} %get-tuple-element.133), channel_id=1, replica_groups=mesh['seq'=64,'tp'=4] {'tp'}, dimensions={1}, use_global_device_ids=true | all-gather | bytes 10240 | tf_op jit(solution)/shard_map/all_gather | solution.py:162
  619.4 0.4 fusion.184
  619.7 0.3 reduce-scatter.35.cloned.1.call-update
  620.1 4.1 convolution_bitcast_fusion
  624.2 1.1 reduce-scatter.27.cloned.1.call-done
  625.3 1.0 copy.95
  626.3 25.2 %reduce-scatter.31.cloned.1.call-done = f32[256,4]{1,0:T(8,128)} async-done(((f32[1024,4]{1,0:T(8,128)}), f32[256,4]{1,0:T(8,128)}) %reduce-scatter.31.cloned.1.call-update) | async-done | bytes 4112
  651.5 1.0 copy.99
  652.4 25.3 %reduce-scatter.35.cloned.1.call-done = f32[256,4]{1,0:T(8,128)} async-done(((f32[1024,4]{1,0:T(8,128)}), f32[256,4]{1,0:T(8,128)}) %reduce-scatter.35.cloned.1.call-update) | async-done | bytes 4112
  677.7 1.0 copy.103
  678.7 25.3 %reduce-scatter.39.cloned.1.call-done = f32[256,4]{1,0:T(8,128)} async-done(((f32[1024,4]{1,0:T(8,128)}), f32[256,4]{1,0:T(8,128)}) %reduce-scatter.39.cloned.1.call-update) | async-done | bytes 4112
  704.0 1.0 copy.107
  705.0 0.6 copy.54
  (186 shorter events, 11.7 us)
Async XLA Ops:
  7.2 588.0 %copy-start = (bf16[1024,1024]{1,0:T(8,128)(2,1)S(1)}, bf16[1024,1024]{1,0:T(8,128)(2,1)}, u32[]{:S(2)}) copy-start(bf16[1024,1024]{1,0:T(8,128)(2,1)} %param.26) | copy-start | bytes 6291460
  7.2 49.4 %copy-start.1 = (bf16[1024,256]{1,0:T(8,128)(2,1)S(1)}, bf16[1024,256]{1,0:T(8,128)(2,1)}, u32[]{:S(2)}) copy-start(bf16[1024,256]{1,0:T(8,128)(2,1)} %param.24) | copy-start | bytes 1572868
  7.2 49.6 %copy-start.2 = (bf16[1024,256]{1,0:T(8,128)(2,1)S(1)}, bf16[1024,256]{1,0:T(8,128)(2,1)}, u32[]{:S(2)}) copy-start(bf16[1024,256]{1,0:T(8,128)(2,1)} %param.23) | copy-start | bytes 1572868
  7.2 468.3 %reduce-scatter.37.cloned.1.call-start = ((), (), s32[]{:S(2)}) async-start(), calls=%async_computation.14 | async-start | bytes 655360
  19.2 26.6 %copy-start.3 = (bf16[1024,256]{1,0:T(8,128)(2,1)S(1)}, bf16[1024,256]{1,0:T(8,128)(2,1)}, u32[]{:S(2)}) copy-start(bf16[1024,256]{1,0:T(8,128)(2,1)} %param.22) | copy-start | bytes 1572868
  45.8 22.3 %copy-start.11 = (f32[2,16]{1,0:T(2,128)S(1)}, f32[2,16]{1,0:T(2,128)}, u32[]{:S(2)}) copy-start(f32[2,16]{1,0:T(2,128)} %param.29) | copy-start | bytes 388
  45.8 22.4 %copy-start.14 = (s32[4]{0:T(128)S(1)}, s32[4]{0:T(128)}, u32[]{:S(2)}) copy-start(s32[4]{0:T(128)} %param.35) | copy-start | bytes 52
  45.8 22.4 %copy-start.8 = (s32[4,4]{1,0:T(4,128)S(1)}, s32[4,4]{1,0:T(4,128)}, u32[]{:S(2)}) copy-start(s32[4,4]{1,0:T(4,128)} %param.37) | copy-start | bytes 196
  45.8 22.6 %copy-start.7 = (s32[4,4]{1,0:T(4,128)S(1)}, s32[4,4]{1,0:T(4,128)}, u32[]{:S(2)}) copy-start(s32[4,4]{1,0:T(4,128)} %param.36) | copy-start | bytes 196
  73.3 2.1 copy-start.10
  73.3 2.1 copy-start.13
  73.3 2.2 copy-start.9
  75.4 108.8 %copy-start.5 = (bf16[4,512,256]{1,2,0:T(8,128)(2,1)}, bf16[4,512,256]{1,2,0:T(8,128)(2,1)S(1)}, u32[]{:S(2)}) copy-start(bf16[4,512,256]{1,2,0:T(8,128)(2,1)S(1)} %copy.48) | copy-start | bytes 3145732
  184.6 3.3 copy-start.6
  184.6 237.2 %copy-start.4 = (bf16[256,1024]{1,0:T(8,128)(2,1)S(1)}, bf16[256,1024]{1,0:T(8,128)(2,1)}, u32[]{:S(2)}) copy-start(bf16[256,1024]{1,0:T(8,128)(2,1)} %param.25) | copy-start | bytes 1572868
  423.0 78.7 %reduce-scatter.33.cloned.1.call-start = ((), (), s32[]{:S(2)}) async-start(), calls=%async_computation.12 | async-start | bytes 655360
  425.7 5.1 copy-start.12
  425.7 102.4 %reduce-scatter.29.cloned.1.call-start = ((), (), s32[]{:S(2)}) async-start(), calls=%async_computation.10 | async-start | bytes 655360
  428.4 125.8 %reduce-scatter.25.cloned.1.call-start = ((), (), s32[]{:S(2)}) async-start(), calls=%async_computation.8 | async-start | bytes 655360
  430.3 195.0 %reduce-scatter.27.cloned.1.call-start = ((), (), s32[]{:S(2)}) async-start(), calls=%async_computation.9 | async-start | bytes 655360
  600.5 51.0 %reduce-scatter.31.cloned.1.call-start = ((), (), s32[]{:S(2)}) async-start(), calls=%async_computation.11 | async-start | bytes 655360
  619.3 58.4 %reduce-scatter.35.cloned.1.call-start = ((), (), s32[]{:S(2)}) async-start(), calls=%async_computation.13 | async-start | bytes 655360
  620.1 84.0 %reduce-scatter.39.cloned.1.call-start = ((), (), s32[]{:S(2)}) async-start(), calls=%async_computation.15 | async-start | bytes 655360
Sparse Core Ops, SparseCore 0:
  423.1 52.3 reduce-scatter.36
  478.1 23.6 reduce-scatter.32
  504.3 23.7 reduce-scatter.28
  530.4 23.7 reduce-scatter.24
  600.6 24.6 reduce-scatter.26
  627.7 23.7 reduce-scatter.30
  654.0 23.7 reduce-scatter.34
  680.3 23.7 reduce-scatter.38
where the time goes:
time: 713 us; the launch traced here: 712 us
  blocking collectives  442 us (62%)
  waiting for transfers between devices  196 us (27%)
  matrix products  34.7 us (5%)
  local copies, waits for them, and re-layouts  18.9 us (3%)
  between operations  14.5 us (2%)
    psum x1, blocking collectives, on_device(): lax.psum((local_total * factor, local_sum * jnp.repeat(factor, HEAD_DIM,...  232 us
    unnamed x16, waiting for transfers between devices  196 us
    pmax x1, blocking collectives, on_device(): peak_all = lax.pmax(local_peak, 'seq')  108 us
    all_gather x4, blocking collectives, on_device(): normed = lax.all_gather(normed_local, 'tp', axis=1, tiled=True)  41.7 us
    all_gather x4, blocking collectives, on_device(): normed_two = lax.all_gather(normed_two_local, 'tp', axis=1, tiled=True)  41.6 us
    unnamed x8, matrix products  21 us
  transfers between devices with their start and end apart: 8, of which 8 were waited for; matrix products, arithmetic and copies ran while one was open for 4% of the time, Pallas kernels for 0%

commit v1 on v0

--- a/solution.py
+++ b/solution.py
@@ -8,6 +8,12 @@
 HEAD_DIM = 64
 STEPS = 4
 epsilon = 1e-05
+
+
+def joined_along(blocks, dim):
+    lengths = list(blocks.shape[1:])
+    lengths[dim] *= blocks.shape[0]
+    return jnp.moveaxis(blocks, 0, dim).reshape(lengths)
 
 
 def rotated(blocks, times):
@@ -159,7 +165,19 @@
         normed_two_local = (middle_local * second_rms[:, None] * gain_second_local).astype(
             jnp.bfloat16
         )
-        normed_two = lax.all_gather(normed_two_local, "tp", axis=1, tiled=True)
+        length = lax.axis_size("tp")
+        pairs = [(i, (i + 1) % length) for i in range(length)]
+        back = [(b, a) for a, b in pairs]
+        lower, upper = ([], [])
+        for lap in range(length - 1):
+            if lap % 2 == 0:
+                lower.append(lax.ppermute(lower[-1] if lower else normed_two_local, "tp", pairs))
+            else:
+                upper.append(lax.ppermute(upper[-1] if upper else normed_two_local, "tp", back))
+        blocks_2 = jnp.stack([*lower[::-1], normed_two_local, *upper])
+        shift = lax.axis_index("tp") - len(lower)
+        blocks_2 = blocks_2[(jnp.arange(length) - shift) % length]
+        normed_two = joined_along(blocks_2, 1)
         gate_part = jnp.dot(normed_two, gate_weight, preferred_element_type=jnp.float32)
         up_part = jnp.dot(normed_two, up_weight, preferred_element_type=jnp.float32)
         activated = (jax.nn.silu(gate_part) * up_part).astype(jnp.bfloat16)

time: 713 us -> 698 us (0.979)
  blocking collectives: 442 us -> 401 us
  starting transfers between devices: 0.51 us -> 15.1 us
  waiting for transfers between devices: 196 us -> 205 us
    all_gather x4 -> x0, blocking collectives: 41.6 us -> none  [on_device(): normed_two = lax.all_gather(normed_two_local, 'tp', axis=1, tiled=True)]
    ppermute x0 -> x12, starting transfers between devices: none -> 14.7 us  [the longest x4 11.7 us: on_device(): lax.ppermute(upper[-1] if upper else normed_two_local, 'tp', back)]
  transfers between devices with their start and end apart: 8 -> 20, of which waited for: 8 -> 9; matrix products, arithmetic and copies ran while one was open for 4% -> 5% of each run, Pallas kernels for 0% -> 0%
where the time goes in v1:
time: 698 us; the launch traced here: 697 us
  blocking collectives  401 us (57%)
  waiting for transfers between devices  205 us (29%)
  matrix products  35.8 us (5%)
  local copies, waits for them, and re-layouts  21.1 us (3%)
  starting transfers between devices  15.1 us (2%)
  between operations  14.5 us (2%)
    psum x1, blocking collectives, on_device(): lax.psum((local_total * factor, local_sum * jnp.repeat(factor, HEAD_DIM,...  232 us
    unnamed x16, waiting for transfers between devices  203 us
    pmax x1, blocking collectives, on_device(): peak_all = lax.pmax(local_peak, 'seq')  108 us
    all_gather x4, blocking collectives, on_device(): normed = lax.all_gather(normed_local, 'tp', axis=1, tiled=True)  41.6 us
    unnamed x8, matrix products  21 us
  transfers between devices with their start and end apart: 20, of which 9 were waited for; matrix products, arithmetic and copies ran while one was open for 5% of the time, Pallas kernels for 0%

profile of v1, /device:TPU:8, one launch (start us, length us, event | category | flops | bytes accessed | tf_op | source)
XLA Modules:
  0.0 697.0 jit_solution(3371172469275032450)
XLA Ops:
  7.3 0.9 fusion.174
  8.7 10.5 %all-reduce.3 = (f32[4]{0:T(128)S(1)}, f32[4]{0:T(128)S(1)}, f32[4]{0:T(128)S(1)}, f32[4]{0:T(128)S(1)}) all-reduce(f32[4]{0:T(128)S(1)} %fusion.94, f32[4]{0:T(128)S(1)} %fusion.106, f32[4]{0:T(128)S(1)} %fusion.102, f32[4]{0:T(128)S(1)} %fusion.98), channel_id=1, replica_groups=mesh['seq'=64,'tp'=4] {'tp'}, use_global_device_ids=true, to_apply=%region_1.0 | all-reduce | flops 16 | bytes 128 | tf_op jit(solution)/shard_map/psum | solution.py:95
  19.2 0.8 dynamic-slice.6
  20.0 10.4 %all_gather.12 = bf16[4,1024]{1,0:T(4,128)(2,1)S(1)} all-gather(bf16[4,256]{1,0:T(4,128)(2,1)S(1)} %get-tuple-element.136), channel_id=1, replica_groups=mesh['seq'=64,'tp'=4] {'tp'}, dimensions={1}, use_global_device_ids=true | all-gather | bytes 10240 | tf_op jit(solution)/shard_map/all_gather | solution.py:100
  30.4 10.4 %all_gather.13 = bf16[4,1024]{1,0:T(4,128)(2,1)S(1)} all-gather(bf16[4,256]{1,0:T(4,128)(2,1)S(1)} %get-tuple-element.137), channel_id=1, replica_groups=mesh['seq'=64,'tp'=4] {'tp'}, dimensions={1}, use_global_device_ids=true | all-gather | bytes 10240 | tf_op jit(solution)/shard_map/all_gather | solution.py:100
  40.8 1.3 fusion.176
  42.1 1.2 fusion.179
  43.3 1.2 convolution_convert_fusion.3
  44.6 1.2 convolution_convert_fusion.2
  45.8 10.4 %all_gather.14 = bf16[4,1024]{1,0:T(4,128)(2,1)S(1)} all-gather(bf16[4,256]{1,0:T(4,128)(2,1)S(1)} %get-tuple-element.138), channel_id=1, replica_groups=mesh['seq'=64,'tp'=4] {'tp'}, dimensions={1}, use_global_device_ids=true | all-gather | bytes 10240 | tf_op jit(solution)/shard_map/all_gather | solution.py:100
  56.6 10.5 %all_gather.15 = bf16[4,1024]{1,0:T(4,128)(2,1)S(1)} all-gather(bf16[4,256]{1,0:T(4,128)(2,1)S(1)} %get-tuple-element.139), channel_id=1, replica_groups=mesh['seq'=64,'tp'=4] {'tp'}, dimensions={1}, use_global_device_ids=true | all-gather | bytes 10240 | tf_op jit(solution)/shard_map/all_gather | solution.py:100
  70.0 1.5 copy.47
  72.2 0.3 fusion.65
  73.9 1.5 copy.48
  75.8 108.2 %all-reduce.1 = (f32[4,4]{1,0:T(4,128)S(1)}, f32[4,4]{1,0:T(4,128)S(1)}, f32[4,4]{1,0:T(4,128)S(1)}, f32[4,4]{1,0:T(4,128)S(1)}) all-reduce(f32[4,4]{1,0:T(4,128)S(1)} %get-tuple-element.78, f32[4,4]{1,0:T(4,128)S(1)} %get-tuple-element.125, f32[4,4]{1,0:T(4,128)S(1)} %get-tuple-element.123, ...), channel_id=1, replica_groups=mesh['seq'=64,'tp'=4] {'seq'}, use_global_device_ids=true, to_apply=%region_40.41 | all-reduce | flops 64 | bytes 512 | tf_op jit(solution)/shard_map/pmax | solution.py:133
  184.2 0.4 fusion.18
  184.8 1.6 fusion.16
  186.5 1.6 fusion.14
  188.3 1.6 fusion.12
  190.6 231.8 %all-reduce = (f32[4,4]{1,0:T(4,128)S(1)}, f32[4,256]{1,0:T(4,128)S(1)}, f32[4,4]{1,0:T(4,128)S(1)}, f32[4,256]{1,0:T(4,128)S(1)}, f32[4,4]{1,0:T(4,128)S(1)}, /...) all-reduce(f32[4,4]{1,0:T(4,128)S(1)} %get-tuple-element.70, ...), channel_id=1, replica_groups=mesh['seq'=64,'tp'=4] {'seq'}, use_global_device_ids=true, to_apply=%region_44.45 | all-reduce | flops 4160 | bytes 33280 | tf_op jit(solution)/shard_map/psum | solution.py:135
  422.9 1.2 convolution_bitcast_fusion.4
  425.6 1.2 convolution_bitcast_fusion.5
  428.2 1.2 convolution_bitcast_fusion.6
  430.2 1.1 convolution_bitcast_fusion.7
  431.9 44.7 %reduce-scatter.37.cloned.1.call-done = f32[256,4]{1,0:T(8,128)} async-done(((f32[1024,4]{1,0:T(8,128)}), f32[256,4]{1,0:T(8,128)}) %reduce-scatter.37.cloned.1.call-update) | async-done | bytes 4112
  476.6 1.0 copy.105
  477.6 25.3 %reduce-scatter.33.cloned.1.call-done = f32[256,4]{1,0:T(8,128)} async-done(((f32[1024,4]{1,0:T(8,128)}), f32[256,4]{1,0:T(8,128)}) %reduce-scatter.33.cloned.1.call-update) | async-done | bytes 4112
  502.8 1.0 copy.101
  503.8 25.3 %reduce-scatter.29.cloned.1.call-done = f32[256,4]{1,0:T(8,128)} async-done(((f32[1024,4]{1,0:T(8,128)}), f32[256,4]{1,0:T(8,128)}) %reduce-scatter.29.cloned.1.call-update) | async-done | bytes 4112
  529.1 1.0 copy.97
  530.1 25.2 %reduce-scatter.25.cloned.1.call-done = f32[256,4]{1,0:T(8,128)} async-done(((f32[1024,4]{1,0:T(8,128)}), f32[256,4]{1,0:T(8,128)}) %reduce-scatter.25.cloned.1.call-update) | async-done | bytes 4112
  555.3 1.0 copy.93
  556.6 8.4 %all-reduce.2 = (f32[4]{0:T(128)S(1)}, f32[4]{0:T(128)S(1)}, f32[4]{0:T(128)S(1)}, f32[4]{0:T(128)S(1)}) all-reduce(f32[4]{0:T(128)S(1)} %get-tuple-element.156, f32[4]{0:T(128)S(1)} %get-tuple-element.54, f32[4]{0:T(128)S(1)} %get-tuple-element.154, f32[4]{0:T(128)S(1)} %get-tuple-element.47), channel_id=1, replica_groups=mesh['seq'=64,'tp'=4] {'tp'}, use_global_device_ids=true, to_apply=%region_48.49 | all-reduce | flops 16 | bytes 128 | tf_op jit(solution)/shard_map/psum | solution.py:163
  565.1 1.3 collective-permute-start
  566.5 2.0 collective-permute-start.2
  568.6 1.4 collective-permute-done
  570.1 0.6 copy.55
  570.7 0.6 copy.56
  571.3 3.1 collective-permute-start.5
  574.4 3.2 collective-permute-start.8
  577.8 0.6 gather_fusion
  578.3 0.4 fusion.177
  578.7 4.1 convolution_bitcast_fusion.3
  582.9 3.3 collective-permute-start.11
  586.2 1.4 collective-permute-start.10
  587.6 0.6 gather_fusion.1
  588.2 0.4 fusion.180
  588.6 4.1 convolution_bitcast_fusion.2
  592.7 0.6 gather_fusion.2
  593.3 0.4 fusion.183
  593.7 4.1 convolution_bitcast_fusion.1
  597.8 0.6 gather_fusion.3
  598.4 0.4 fusion.186
  598.8 0.3 reduce-scatter.35.cloned.1.call-update
  599.2 4.1 convolution_bitcast_fusion
  603.3 6.6 reduce-scatter.27.cloned.1.call-done
  609.8 1.0 copy.95
  610.8 25.2 %reduce-scatter.31.cloned.1.call-done = f32[256,4]{1,0:T(8,128)} async-done(((f32[1024,4]{1,0:T(8,128)}), f32[256,4]{1,0:T(8,128)}) %reduce-scatter.31.cloned.1.call-update) | async-done | bytes 4112
  636.0 1.0 copy.99
  636.9 25.3 %reduce-scatter.35.cloned.1.call-done = f32[256,4]{1,0:T(8,128)} async-done(((f32[1024,4]{1,0:T(8,128)}), f32[256,4]{1,0:T(8,128)}) %reduce-scatter.35.cloned.1.call-update) | async-done | bytes 4112
  662.2 1.0 copy.103
  663.2 25.3 %reduce-scatter.39.cloned.1.call-done = f32[256,4]{1,0:T(8,128)} async-done(((f32[1024,4]{1,0:T(8,128)}), f32[256,4]{1,0:T(8,128)}) %reduce-scatter.39.cloned.1.call-update) | async-done | bytes 4112
  688.5 1.0 copy.107
  689.5 0.6 copy.54
  (214 shorter events, 13.5 us)
Async XLA Ops:
  7.2 571.2 %copy-start = (bf16[1024,1024]{1,0:T(8,128)(2,1)S(1)}, bf16[1024,1024]{1,0:T(8,128)(2,1)}, u32[]{:S(2)}) copy-start(bf16[1024,1024]{1,0:T(8,128)(2,1)} %param.26) | copy-start | bytes 6291460
  7.2 49.0 %copy-start.1 = (bf16[1024,256]{1,0:T(8,128)(2,1)S(1)}, bf16[1024,256]{1,0:T(8,128)(2,1)}, u32[]{:S(2)}) copy-start(bf16[1024,256]{1,0:T(8,128)(2,1)} %param.23) | copy-start | bytes 1572868
  7.2 49.2 %copy-start.2 = (bf16[1024,256]{1,0:T(8,128)(2,1)S(1)}, bf16[1024,256]{1,0:T(8,128)(2,1)}, u32[]{:S(2)}) copy-start(bf16[1024,256]{1,0:T(8,128)(2,1)} %param.24) | copy-start | bytes 1572868
  7.2 469.4 %reduce-scatter.37.cloned.1.call-start = ((), (), s32[]{:S(2)}) async-start(), calls=%async_computation.14 | async-start | bytes 655360
  40.8 26.5 %copy-start.3 = (bf16[1024,256]{1,0:T(8,128)(2,1)S(1)}, bf16[1024,256]{1,0:T(8,128)(2,1)}, u32[]{:S(2)}) copy-start(bf16[1024,256]{1,0:T(8,128)(2,1)} %param.22) | copy-start | bytes 1572868
  56.2 12.0 %copy-start.7 = (s32[4,4]{1,0:T(4,128)S(1)}, s32[4,4]{1,0:T(4,128)}, u32[]{:S(2)}) copy-start(s32[4,4]{1,0:T(4,128)} %param.37) | copy-start | bytes 196
  56.4 12.7 %copy-start.10 = (f32[2,16]{1,0:T(2,128)S(1)}, f32[2,16]{1,0:T(2,128)}, u32[]{:S(2)}) copy-start(f32[2,16]{1,0:T(2,128)} %param.29) | copy-start | bytes 388
  56.4 12.8 %copy-start.6 = (s32[4,4]{1,0:T(4,128)S(1)}, s32[4,4]{1,0:T(4,128)}, u32[]{:S(2)}) copy-start(s32[4,4]{1,0:T(4,128)} %param.36) | copy-start | bytes 196
  72.2 1.6 copy-start.13
  73.1 2.3 copy-start.8
  73.1 2.4 copy-start.9
  73.1 2.4 copy-start.12
  75.4 108.8 %copy-start.5 = (bf16[4,512,256]{1,2,0:T(8,128)(2,1)}, bf16[4,512,256]{1,2,0:T(8,128)(2,1)S(1)}, u32[]{:S(2)}) copy-start(bf16[4,512,256]{1,2,0:T(8,128)(2,1)S(1)} %copy.48) | copy-start | bytes 3145732
  184.6 238.3 %copy-start.4 = (bf16[256,1024]{1,0:T(8,128)(2,1)S(1)}, bf16[256,1024]{1,0:T(8,128)(2,1)}, u32[]{:S(2)}) copy-start(bf16[256,1024]{1,0:T(8,128)(2,1)} %param.25) | copy-start | bytes 1572868
  424.1 78.7 %reduce-scatter.33.cloned.1.call-start = ((), (), s32[]{:S(2)}) async-start(), calls=%async_computation.12 | async-start | bytes 655360
  426.8 5.1 copy-start.11
  426.8 102.4 %reduce-scatter.29.cloned.1.call-start = ((), (), s32[]{:S(2)}) async-start(), calls=%async_computation.10 | async-start | bytes 655360
  429.4 125.8 %reduce-scatter.25.cloned.1.call-start = ((), (), s32[]{:S(2)}) async-start(), calls=%async_computation.8 | async-start | bytes 655360
  431.4 178.4 %reduce-scatter.27.cloned.1.call-start = ((), (), s32[]{:S(2)}) async-start(), calls=%async_computation.9 | async-start | bytes 655360
  565.1 4.8 collective-permute-start
  566.5 7.9 %collective-permute-start.2 = (bf16[4,256]{1,0:T(4,128)(2,1)S(1)}, bf16[4,256]{1,0:T(4,128)(2,1)S(1)}, u32[]{:S(2)}, u32[]{:S(2)}) collective-permute-start(bf16[4,256]{1,0:T(4,128)(2,1)S(1)} %get-tuple-element.130), channel_id=1, source_target_pairs={{1,0},{2,1},{3,2},{0,3},{5,4},{6,5},{7,6},{4,7},{9,8},{10,9},{11,1... | collective-permute-start | bytes 6152 | tf_op jit(solution)/shard_map/ppermute | solution.py:176
  568.5 9.2 %collective-permute-start.3 = (bf16[4,256]{1,0:T(4,128)(2,1)S(1)}, bf16[4,256]{1,0:T(4,128)(2,1)S(1)}, u32[]{:S(2)}, u32[]{:S(2)}) collective-permute-start(bf16[4,256]{1,0:T(4,128)(2,1)S(1)} %get-tuple-element.131), channel_id=1, source_target_pairs={{0,1},{1,2},{2,3},{3,0},{4,5},{5,6},{6,7},{7,4},{8,9},{9,10},{10,1... | collective-permute-start | bytes 6152 | tf_op jit(solution)/shard_map/ppermute | solution.py:174
  569.9 7.7 %collective-permute-start.1 = (bf16[4,256]{1,0:T(4,128)(2,1)S(1)}, bf16[4,256]{1,0:T(4,128)(2,1)S(1)}, u32[]{:S(2)}, u32[]{:S(2)}) collective-permute-start(bf16[4,256]{1,0:T(4,128)(2,1)S(1)} %collective-permute-done), channel_id=1, source_target_pairs={{0,1},{1,2},{2,3},{3,0},{4,5},{5,6},{6,7},{7,4},{8,9},{9,10},{10,1... | collective-permute-start | bytes 6152 | tf_op jit(solution)/shard_map/ppermute | solution.py:174
  571.3 11.6 %collective-permute-start.5 = (bf16[4,256]{1,0:T(4,128)(2,1)S(1)}, bf16[4,256]{1,0:T(4,128)(2,1)S(1)}, u32[]{:S(2)}, u32[]{:S(2)}) collective-permute-start(bf16[4,256]{1,0:T(4,128)(2,1)S(1)} %get-tuple-element.131), channel_id=1, source_target_pairs={{1,0},{2,1},{3,2},{0,3},{5,4},{6,5},{7,6},{4,7},{9,8},{10,9},{11,1... | collective-permute-start | bytes 6152 | tf_op jit(solution)/shard_map/ppermute | solution.py:176
  574.4 11.8 %collective-permute-start.6 = (bf16[4,256]{1,0:T(4,128)(2,1)S(1)}, bf16[4,256]{1,0:T(4,128)(2,1)S(1)}, u32[]{:S(2)}, u32[]{:S(2)}) collective-permute-start(bf16[4,256]{1,0:T(4,128)(2,1)S(1)} %get-tuple-element.132), channel_id=1, source_target_pairs={{0,1},{1,2},{2,3},{3,0},{4,5},{5,6},{6,7},{7,4},{8,9},{9,10},{10,1... | collective-permute-start | bytes 6152 | tf_op jit(solution)/shard_map/ppermute | solution.py:174
  574.4 18.3 %collective-permute-start.8 = (bf16[4,256]{1,0:T(4,128)(2,1)S(1)}, bf16[4,256]{1,0:T(4,128)(2,1)S(1)}, u32[]{:S(2)}, u32[]{:S(2)}) collective-permute-start(bf16[4,256]{1,0:T(4,128)(2,1)S(1)} %get-tuple-element.132), channel_id=1, source_target_pairs={{1,0},{2,1},{3,2},{0,3},{5,4},{6,5},{7,6},{4,7},{9,8},{10,9},{11,1... | collective-permute-start | bytes 6152 | tf_op jit(solution)/shard_map/ppermute | solution.py:176
  577.6 8.6 %collective-permute-start.9 = (bf16[4,256]{1,0:T(4,128)(2,1)S(1)}, bf16[4,256]{1,0:T(4,128)(2,1)S(1)}, u32[]{:S(2)}, u32[]{:S(2)}) collective-permute-start(bf16[4,256]{1,0:T(4,128)(2,1)S(1)} %get-tuple-element.133), channel_id=1, source_target_pairs={{0,1},{1,2},{2,3},{3,0},{4,5},{5,6},{6,7},{7,4},{8,9},{9,10},{10,1... | collective-permute-start | bytes 6152 | tf_op jit(solution)/shard_map/ppermute | solution.py:174
  577.6 10.0 %collective-permute-start.4 = (bf16[4,256]{1,0:T(4,128)(2,1)S(1)}, bf16[4,256]{1,0:T(4,128)(2,1)S(1)}, u32[]{:S(2)}, u32[]{:S(2)}) collective-permute-start(bf16[4,256]{1,0:T(4,128)(2,1)S(1)} %collective-permute-done.3), channel_id=1, source_target_pairs={{0,1},{1,2},{2,3},{3,0},{4,5},{5,6},{6,7},{7,4},{8,9},{9,10},{10,1... | collective-permute-start | bytes 6152 | tf_op jit(solution)/shard_map/ppermute | solution.py:174
  582.8 53.1 %reduce-scatter.31.cloned.1.call-start = ((), (), s32[]{:S(2)}) async-start(), calls=%async_computation.11 | async-start | bytes 655360
  582.9 14.8 %collective-permute-start.11 = (bf16[4,256]{1,0:T(4,128)(2,1)S(1)}, bf16[4,256]{1,0:T(4,128)(2,1)S(1)}, u32[]{:S(2)}, u32[]{:S(2)}) collective-permute-start(bf16[4,256]{1,0:T(4,128)(2,1)S(1)} %get-tuple-element.133), channel_id=1, source_target_pairs={{1,0},{2,1},{3,2},{0,3},{5,4},{6,5},{7,6},{4,7},{9,8},{10,9},{11,1... | collective-permute-start | bytes 6152 | tf_op jit(solution)/shard_map/ppermute | solution.py:176
  586.2 6.5 collective-permute-start.7
  586.2 11.5 %collective-permute-start.10 = (bf16[4,256]{1,0:T(4,128)(2,1)S(1)}, bf16[4,256]{1,0:T(4,128)(2,1)S(1)}, u32[]{:S(2)}, u32[]{:S(2)}) collective-permute-start(bf16[4,256]{1,0:T(4,128)(2,1)S(1)} %collective-permute-done.9), channel_id=1, source_target_pairs={{0,1},{1,2},{2,3},{3,0},{4,5},{5,6},{6,7},{7,4},{8,9},{9,10},{10,1... | collective-permute-start | bytes 6152 | tf_op jit(solution)/shard_map/ppermute | solution.py:174
  598.4 63.9 %reduce-scatter.35.cloned.1.call-start = ((), (), s32[]{:S(2)}) async-start(), calls=%async_computation.13 | async-start | bytes 655360
  599.1 89.4 %reduce-scatter.39.cloned.1.call-start = ((), (), s32[]{:S(2)}) async-start(), calls=%async_computation.15 | async-start | bytes 655360
Sparse Core Ops, SparseCore 0:
  424.2 52.3 reduce-scatter.36
  479.1 23.6 reduce-scatter.32
  505.4 23.7 reduce-scatter.28
  531.5 23.7 reduce-scatter.24
  582.9 26.8 reduce-scatter.26
  612.2 23.7 reduce-scatter.30
  638.5 23.7 reduce-scatter.34
  664.8 23.7 reduce-scatter.38
